TPU v7x, 768 devices: a whole 4x8x12 slice. The times are simulated.
768 devices in a mesh: wide: 32 (over x, y_lo, core), pair: 12 (over z), sub: 2 (over y_hi).
Axes of the slice: x: 4, y: 8 (y_hi: 2, y_lo: 4; y = y_hi * 4 + y_lo), z: 12, core: 2. Of those that a mesh axis runs over, the one named last changes fastest.
Arguments:
- orbitals: bfloat16 [6, 64, 160, 160], P(None, ('wide', 'sub')), may hold values from -0.5 to 0.5
- couplings: bfloat16 [24, 160, 160], P('pair'), may hold values from -6 to 6
- blocks: int32 [24, 2], P('pair'), may hold values from 0 to 5, as said below
- partner: int32 [24], P('pair'), may hold values from 0 to 23, as said below
Outputs:
- self_energy: bfloat16 [24, 64, 160, 160], P('pair', ('wide', 'sub'))
Inputs may be any that keep to these rules, and one draw needn't show every extreme that they name: blocks[partner[b]] is blocks[b] with its two entries swapped, and the two entries of a row differ. partner is an involution without fixed points; the partner of a block lies among the 2 blocks of the index of pair that is half the pair axis away.
All inputs are finite; a program needn't handle non-finite values.
Results may differ from a plain program's by a relative error of at most 0.014.
Values may be sent and summed in bfloat16 or wider, within the bound.
No kernel may reach another device: no remote copies, remote signals or barrier semaphores. Data moves between devices by JAX's collectives and lax.ppermute only.
A program may use at most 32 MiB of HBM per device.

v0:
```python
import functools

import jax
import jax.numpy as jnp
from jax import lax
from jax.experimental import pallas as pl
from jax.experimental.pallas import tpu as pltpu
from jax.sharding import PartitionSpec as P


LANES = 128
ROWS = 8
VMEM = pl.BlockSpec(memory_space=pltpu.VMEM)
SMEM = pl.BlockSpec(memory_space=pltpu.SMEM)


def matmul(left, right):
    return jnp.dot(left, right, preferred_element_type=jnp.float32)


def matmul_t(left, right):
    return lax.dot_general(
        left, right, (((1,), (1,)), ((), ())), preferred_element_type=jnp.float32
    )


def pack(first, second):
    half = first.shape[0] // 2
    rest = jnp.concatenate(
        [
            first[:half, LANES:],
            first[half:, LANES:],
            second[:half, LANES:],
            second[half:, LANES:],
        ],
        axis=1,
    )
    return jnp.concatenate([first[:, :LANES], second[:, :LANES], rest], axis=0)


def unpack(packed, order, b):
    half = order // 2
    width = order - LANES
    rest = packed[2 * order : 2 * order + half, :]
    at = 2 * b * width
    tail = jnp.concatenate(
        [rest[:, at : at + width], rest[:, at + width : at + 2 * width]], axis=0
    )
    return jnp.concatenate([packed[b * order : (b + 1) * order, :], tail], axis=1)


def send_kernel(couplings, out):
    out[...] = pack(couplings[0], couplings[1])


def direct_kernel(blocks, partner, orbitals, couplings, out, factors, arriving, crossed):
    first = lax.rem(partner[0], 2)
    results = []
    for b in range(2):
        left = orbitals[blocks[b, 0]]
        right = orbitals[blocks[b, 1]]
        slot = first if b == 0 else 1 - first
        for side, factor in enumerate((left, right)):
            factors[2 * b + side] = factor
            arriving[2 * slot + side] = factor
        inner = matmul(left, couplings[b]).astype(jnp.bfloat16)
        results.append(matmul_t(inner, right))
    out[...] = pack(*results).astype(jnp.bfloat16)
    crossed[...] = jnp.full(crossed.shape, first, jnp.int32)


def mirror_kernel(factors, crossed, shifted, direct, out):
    results = []
    for b in range(2):
        coupling = unpack(shifted, factors.shape[1], b)
        across = matmul(factors[2 * b + 1], coupling).astype(jnp.bfloat16)
        results.append(matmul_t(factors[2 * b], across))
    arrived = pack(*results)
    order = factors.shape[1]
    swap = jnp.broadcast_to(crossed[0:1, :], arrived.shape) > 0
    half = (order - LANES) * 2
    rest = arrived[2 * order :]
    turned = jnp.concatenate(
        [
            arrived[order : 2 * order],
            arrived[:order],
            jnp.concatenate([rest[:, half:], rest[:, :half]], axis=1),
        ],
        axis=0,
    )
    mirror = jnp.where(swap, turned, arrived)
    used = direct.shape[0] // ROWS
    both = jnp.concatenate(
        [
            direct[...].astype(jnp.float32).reshape(used, ROWS, LANES),
            mirror.reshape(used, ROWS, LANES),
        ],
        axis=1,
    )
    out[:used] = both.astype(jnp.bfloat16)
    out[used:] = jnp.zeros((out.shape[0] - used, 2 * ROWS, LANES), jnp.bfloat16)


def convolve_kernel(tile, incoming, out, first, second):
    count = incoming.shape[0]
    both = incoming[...].astype(jnp.float32)
    first[...] = both[:, :ROWS]
    second[...] = both[:, ROWS:]
    scale = count ** (-0.5)
    for e0 in range(0, count, tile):
        totals = [None] * tile
        for t0 in range(0, e0 + tile, tile):
            lhs = [first[t0 + k] for k in range(tile)]
            base = e0 - t0 - tile + 1
            rhs = [
                second[base + k] if base + k >= 0 else None for k in range(2 * tile - 1)
            ]
            for de in range(tile):
                for dt in range(tile):
                    other = rhs[de - dt + tile - 1]
                    if other is None:
                        continue
                    term = lhs[dt] * other
                    totals[de] = term if totals[de] is None else totals[de] + term
        for de in range(0, tile, 2):
            pair = jnp.concatenate([totals[de], totals[de + 1]], axis=0) * scale
            out[pl.ds((e0 + de) * ROWS, 2 * ROWS), :] = pair.astype(jnp.bfloat16)


def screen_kernel(factors, packed, out, held, sems):
    copies = []
    for b in range(2):
        polar = unpack(packed, held.shape[1], b)
        screened = matmul(factors[2 * b], polar).astype(jnp.bfloat16)
        held[b] = matmul_t(screened, factors[2 * b + 1]).astype(jnp.bfloat16)
        copy = pltpu.make_async_copy(held.at[b], out.at[b], sems.at[b])
        copy.start()
        copies.append(copy)
    for copy in copies:
        copy.wait()


def onchip(value):
    return pltpu.with_memory_space_constraint(value, pltpu.VMEM)


def per_device(orbitals, couplings, blocks, partner):
    axes = ("wide", "sub")
    energies = lax.axis_size("wide") * lax.axis_size("sub")
    pairs = lax.axis_size("pair")
    order = couplings.shape[1]
    packed_rows = 2 * order * order // LANES
    packed = pltpu.VMEM((packed_rows, LANES), jnp.bfloat16)
    leaving = pl.pallas_call(
        send_kernel,
        out_shape=packed,
        in_specs=[VMEM],
        out_specs=VMEM,
        name="send",
    )(couplings)
    near = pairs // 2
    early = lax.axis_index("pair") < near
    from_late = lax.ppermute(leaving, "pair", [(i + near, i) for i in range(near)])
    from_early = lax.ppermute(leaving, "pair", [(i, i + near) for i in range(near)])
    sites = orbitals.reshape(orbitals.shape[0], order, order)
    chosen = pltpu.VMEM((4, order, order), jnp.bfloat16)
    direct, factors, arriving, crossed = pl.pallas_call(
        direct_kernel,
        out_shape=[packed, chosen, chosen, pltpu.VMEM((ROWS, LANES), jnp.int32)],
        in_specs=[SMEM, SMEM, VMEM, VMEM],
        out_specs=[VMEM] * 4,
        name="direct",
    )(blocks, partner, sites, couplings)
    result = pltpu.VMEM((energies * ROWS, LANES), jnp.bfloat16)

    def polarize(polar, shifted, direct, arriving, crossed):
        outgoing = pl.pallas_call(
            mirror_kernel,
            out_shape=pltpu.VMEM((energies, 2 * ROWS, LANES), jnp.bfloat16),
            in_specs=[VMEM] * 4,
            out_specs=VMEM,
            name="mirror",
        )(onchip(arriving), onchip(crossed), onchip(shifted), onchip(direct))
        incoming = lax.all_to_all(outgoing, axes, split_axis=0, concat_axis=0, tiled=True)
        return pl.pallas_call(
            functools.partial(convolve_kernel, 8),
            out_shape=result,
            in_specs=[VMEM],
            out_specs=VMEM,
            scratch_shapes=[pltpu.VMEM((energies, ROWS, LANES), jnp.float32)] * 2,
            name="convolve",
        )(onchip(incoming))

    def keep(polar, *_):
        return polar

    polar = jnp.zeros((energies * ROWS, LANES), jnp.bfloat16)
    polar = lax.cond(early, polarize, keep, polar, from_late, direct, arriving, crossed)
    polar = lax.cond(early, keep, polarize, polar, from_early, direct, arriving, crossed)
    returned = lax.all_to_all(
        polar.reshape(energies, ROWS, LANES), axes, split_axis=0, concat_axis=0, tiled=True
    )
    screened = pl.pallas_call(
        screen_kernel,
        out_shape=jax.ShapeDtypeStruct(couplings.shape, jnp.bfloat16),
        in_specs=[VMEM, VMEM],
        out_specs=pl.BlockSpec(memory_space=pl.ANY),
        scratch_shapes=[
            pltpu.VMEM(couplings.shape, jnp.bfloat16),
            pltpu.SemaphoreType.DMA((2,)),
        ],
        name="screen",
    )(onchip(factors), onchip(returned.reshape(energies * ROWS, LANES)))
    return screened.reshape(couplings.shape[0], 1, order, order)


def solution(mesh):
    placed = (
        P(None, ("wide", "sub"), None, None),
        P("pair", None, None),
        P("pair", None),
        P("pair"),
    )
    return jax.shard_map(
        per_device,
        mesh=mesh,
        in_specs=placed,
        out_specs=P("pair", ("wide", "sub"), None, None),
        check_vma=False,
    )
```

profile of v0, /device:TPU:64, one launch (start us, length us, event | category | flops | bytes accessed | tf_op | source)
XLA Modules:
  0.0 61.9 jit_solution(17377478926170747855)
XLA Ops:
  0.0 1.0 %send.1 = bf16[400,128]{1,0:T(8,128)(2,1)S(1)} custom-call(bf16[2,160,160]{2,1,0:T(8,128)(2,1)} %couplings.3), custom_call_target="tpu_custom_call" | custom-call | tf_op jit(solution)/shard_map/send/pallas_call | solution.py:154
  1.0 1.3 %collective-permute-start.1 = (bf16[400,128]{1,0:T(8,128)(2,1)S(1)}, bf16[400,128]{1,0:T(8,128)(2,1)S(1)}, u32[]{:S(2)}, u32[]{:S(2)}) collective-permute-start(bf16[400,128]{1,0:T(8,128)(2,1)S(1)} %send.1), channel_id=1, source_target_pairs={{12,0},{14,2},{16,4},{18,6},{20,8},{22,10},{13,1},{15,3},{17,5},{1... | collective-permute-start | bytes 307208 | tf_op jit(solution)/shard_map/ppermute | solution.py:163
  2.3 14.2 %collective-permute-start = (bf16[400,128]{1,0:T(8,128)(2,1)S(1)}, bf16[400,128]{1,0:T(8,128)(2,1)S(1)}, u32[]{:S(2)}, u32[]{:S(2)}) collective-permute-start(bf16[400,128]{1,0:T(8,128)(2,1)S(1)} %send.1), channel_id=1, source_target_pairs={{0,12},{2,14},{4,16},{6,18},{8,20},{10,22},{1,13},{3,15},{5,17},{7... | collective-permute-start | bytes 307208 | tf_op jit(solution)/shard_map/ppermute | solution.py:164
  16.6 1.5 %direct.1 = (bf16[400,128]{1,0:T(8,128)(2,1)S(1)}, bf16[4,160,160]{2,1,0:T(8,128)(2,1)S(1)}, bf16[4,160,160]{2,1,0:T(8,128)(2,1)S(1)}, s32[8,128]{1,0:T(8,128)S(1)}) custom-call(s32[2,2]{1,0:T(2,128)} %blocks.1, s32[2]{0:T(128)} %partner.1, bf16[6,160,160]{2,1,0:T(8,128)(2,1)} %bitcast.8, bf16[2,160,160]{2,1,0:T(8,128)(2,1)} %couplings.3), custom_call_target="tpu_custom_call" | custom-call | tf_op jit(solution)/shard_map/direct/pallas_call | solution.py:167
  18.1 1.7 %collective-permute-done.1 = bf16[400,128]{1,0:T(8,128)(2,1)S(1)} collective-permute-done((bf16[400,128]{1,0:T(8,128)(2,1)S(1)}, bf16[400,128]{1,0:T(8,128)(2,1)S(1)}, u32[]{:S(2)}, u32[]{:S(2)}) %collective-permute-start.1) | collective-permute-done | bytes 102432 | tf_op jit(solution)/shard_map/ppermute | solution.py:163
  19.8 25.8 %conditional.2 = (bf16[512,128]{1,0:T(8,128)(2,1)S(1)}) conditional(s32[]{:T(128)} %convert_element_type.4, () %tuple.18, (bf16[4,160,160]{2,1,0:T(8,128)(2,1)S(1)}, s32[8,128]{1,0:T(8,128)S(1)}, bf16[400,128]{1,0:T(8,128)(2,1)S(1)}, bf16[400,128]{1,0:T(8,128)(2,1)S(1)}) %tuple.19), branch_computations={%region_0.0_spmd, %region_1.0_spmd} | conditional | bytes 524296 | solution.py:198
  19.8 0.6 mirror.2
  20.4 24.6 %all_to_all.13.incoming = bf16[64,16,128]{2,1,0:T(8,128)(2,1)S(1)} all-to-all(bf16[64,16,128]{2,1,0:T(8,128)(2,1)S(1)} %mirror.2), channel_id=1, replica_groups=mesh['wide'=32,'pair'=12,'sub'=2] {'wide','sub'}, dimensions={0} | all-to-all | bytes 524288 | tf_op jit(solution)/shard_map/cond/branch_1_fun/all_to_all | solution.py:184
  45.0 0.6 convolve.2
  45.6 0.0 collective-permute-done
  45.6 15.2 %all_to_all.15 = bf16[64,8,128]{2,1,0:T(8,128)(2,1)S(1)} all-to-all(bf16[64,8,128]{2,1,0:T(8,128)(2,1)S(1)} %bitcast.7), channel_id=1, replica_groups=mesh['wide'=32,'pair'=12,'sub'=2] {'wide','sub'}, dimensions={0} | all-to-all | bytes 262144 | tf_op jit(solution)/shard_map/all_to_all | solution.py:200
  60.8 1.1 %screen.1 = bf16[2,160,160]{2,1,0:T(8,128)(2,1)} custom-call(bf16[4,160,160]{2,1,0:T(8,128)(2,1)S(1)} %get-tuple-element.40.factors, bf16[512,128]{1,0:T(8,128)(2,1)S(1)} %bitcast.6), custom_call_target="tpu_custom_call" | custom-call | tf_op jit(solution)/shard_map/screen/pallas_call | solution.py:203
  (1 shorter events, 0.0 us)
Async XLA Ops:
  1.0 18.8 %collective-permute-start.1 = (bf16[400,128]{1,0:T(8,128)(2,1)S(1)}, bf16[400,128]{1,0:T(8,128)(2,1)S(1)}, u32[]{:S(2)}, u32[]{:S(2)}) collective-permute-start(bf16[400,128]{1,0:T(8,128)(2,1)S(1)} %send.1), channel_id=1, source_target_pairs={{12,0},{14,2},{16,4},{18,6},{20,8},{22,10},{13,1},{15,3},{17,5},{1... | collective-permute-start | bytes 307208 | tf_op jit(solution)/shard_map/ppermute | solution.py:163
  2.3 43.3 %collective-permute-start = (bf16[400,128]{1,0:T(8,128)(2,1)S(1)}, bf16[400,128]{1,0:T(8,128)(2,1)S(1)}, u32[]{:S(2)}, u32[]{:S(2)}) collective-permute-start(bf16[400,128]{1,0:T(8,128)(2,1)S(1)} %send.1), channel_id=1, source_target_pairs={{0,12},{2,14},{4,16},{6,18},{8,20},{10,22},{1,13},{3,15},{5,17},{7... | collective-permute-start | bytes 307208 | tf_op jit(solution)/shard_map/ppermute | solution.py:164
where the time goes:
time: 62.1 us; the launch traced here: 61.9 us
  blocking collectives  39.8 us (64%)
  starting transfers between devices  15.5 us (25%)
  Pallas kernels  4.76 us (8%)
  waiting for transfers between devices  1.73 us (3%)
    all_to_all x1, blocking collectives, polarize(): lax.all_to_all(outgoing, axes, split_axis=0, concat_axis=0, tiled=True)  24.6 us
    all_to_all x1, blocking collectives, per_device(): lax.all_to_all(polar.reshape(energies, ROWS, LANES), axes, split_axis=0,...  15.2 us
    ppermute x1, starting transfers between devices, per_device(): lax.ppermute(leaving, 'pair', [(i, i + near) for i in range(near)])  14.2 us
    ppermute x1, waiting for transfers between devices, per_device(): lax.ppermute(leaving, 'pair', [(i + near, i) for i in range(near)])  1.73 us
    pallas_call x1, Pallas kernels, per_device(): pl.pallas_call(direct_kernel, out_shape=[packed, chosen, chosen, pltpu.VM...  1.48 us
    ppermute x1, starting transfers between devices, per_device(): lax.ppermute(leaving, 'pair', [(i + near, i) for i in range(near)])  1.29 us
  transfers between devices with their start and end apart: 2, of which 1 were waited for; matrix products, arithmetic and copies ran while one was open for 0% of the time, Pallas kernels for 4%

commit v1 on v0

--- a/solution.py
+++ b/solution.py
@@ -5,10 +5,12 @@
 from jax import lax
 from jax.experimental import pallas as pl
 from jax.experimental.pallas import tpu as pltpu
+from jax.sharding import Mesh
 from jax.sharding import PartitionSpec as P
 
 
 LANES = 128
+CHIPS_X = 4
 ROWS = 8
 VMEM = pl.BlockSpec(memory_space=pltpu.VMEM)
 SMEM = pl.BlockSpec(memory_space=pltpu.SMEM)
@@ -101,19 +103,24 @@
     out[used:] = jnp.zeros((out.shape[0] - used, 2 * ROWS, LANES), jnp.bfloat16)
 
 
-def convolve_kernel(tile, incoming, out, first, second):
+def convolve_kernel(tile, inner, incoming, out, first, second):
     count = incoming.shape[0]
     both = incoming[...].astype(jnp.float32)
     first[...] = both[:, :ROWS]
     second[...] = both[:, ROWS:]
     scale = count ** (-0.5)
+
+    def slot(energy):
+        return energy % inner * (count // inner) + energy // inner
+
     for e0 in range(0, count, tile):
         totals = [None] * tile
         for t0 in range(0, e0 + tile, tile):
-            lhs = [first[t0 + k] for k in range(tile)]
+            lhs = [first[slot(t0 + k)] for k in range(tile)]
             base = e0 - t0 - tile + 1
             rhs = [
-                second[base + k] if base + k >= 0 else None for k in range(2 * tile - 1)
+                second[slot(base + k)] if base + k >= 0 else None
+                for k in range(2 * tile - 1)
             ]
             for de in range(tile):
                 for dt in range(tile):
@@ -122,9 +129,9 @@
                         continue
                     term = lhs[dt] * other
                     totals[de] = term if totals[de] is None else totals[de] + term
-        for de in range(0, tile, 2):
-            pair = jnp.concatenate([totals[de], totals[de + 1]], axis=0) * scale
-            out[pl.ds((e0 + de) * ROWS, 2 * ROWS), :] = pair.astype(jnp.bfloat16)
+        for de in range(tile):
+            total = (totals[de] * scale).astype(jnp.bfloat16)
+            out[pl.ds(slot(e0 + de) * ROWS, ROWS), :] = total
 
 
 def screen_kernel(factors, packed, out, held, sems):
@@ -145,8 +152,8 @@
 
 
 def per_device(orbitals, couplings, blocks, partner):
-    axes = ("wide", "sub")
-    energies = lax.axis_size("wide") * lax.axis_size("sub")
+    axes = ("inside", "sub", "x")
+    energies = lax.axis_size(axes)
     pairs = lax.axis_size("pair")
     order = couplings.shape[1]
     packed_rows = 2 * order * order // LANES
@@ -183,7 +190,7 @@
         )(onchip(arriving), onchip(crossed), onchip(shifted), onchip(direct))
         incoming = lax.all_to_all(outgoing, axes, split_axis=0, concat_axis=0, tiled=True)
         return pl.pallas_call(
-            functools.partial(convolve_kernel, 8),
+            functools.partial(convolve_kernel, 8, energies // lax.axis_size("x")),
             out_shape=result,
             in_specs=[VMEM],
             out_specs=VMEM,
@@ -215,16 +222,22 @@
 
 
 def solution(mesh):
+    sizes = mesh.shape
+    split = Mesh(
+        mesh.devices.reshape(CHIPS_X, -1, sizes["pair"], sizes["sub"]),
+        ("x", "inside", "pair", "sub"),
+    )
+    energy = ("x", "inside", "sub")
     placed = (
-        P(None, ("wide", "sub"), None, None),
+        P(None, energy, None, None),
         P("pair", None, None),
         P("pair", None),
         P("pair"),
     )
     return jax.shard_map(
         per_device,
-        mesh=mesh,
+        mesh=split,
         in_specs=placed,
-        out_specs=P("pair", ("wide", "sub"), None, None),
+        out_specs=P("pair", energy, None, None),
         check_vma=False,
     )

time: 62.1 us -> 61.1 us (0.984)
  blocking collectives: 39.8 us -> 38.8 us
where the time goes in v1:
time: 61.1 us; the launch traced here: 60.9 us
  blocking collectives  38.8 us (64%)
  starting transfers between devices  15.5 us (25%)
  Pallas kernels  4.77 us (8%)
  waiting for transfers between devices  1.73 us (3%)
    all_to_all x1, blocking collectives, polarize(): lax.all_to_all(outgoing, axes, split_axis=0, concat_axis=0, tiled=True)  24.1 us
    all_to_all x1, blocking collectives, per_device(): lax.all_to_all(polar.reshape(energies, ROWS, LANES), axes, split_axis=0,...  14.7 us
    ppermute x1, starting transfers between devices, per_device(): lax.ppermute(leaving, 'pair', [(i, i + near) for i in range(near)])  14.2 us
    ppermute x1, waiting for transfers between devices, per_device(): lax.ppermute(leaving, 'pair', [(i + near, i) for i in range(near)])  1.73 us
    pallas_call x1, Pallas kernels, per_device(): pl.pallas_call(direct_kernel, out_shape=[packed, chosen, chosen, pltpu.VM...  1.48 us
    ppermute x1, starting transfers between devices, per_device(): lax.ppermute(leaving, 'pair', [(i + near, i) for i in range(near)])  1.29 us
  transfers between devices with their start and end apart: 2, of which 1 were waited for; matrix products, arithmetic and copies ran while one was open for 0% of the time, Pallas kernels for 4%

profile of v1, /device:TPU:64, one launch (start us, length us, event | category | flops | bytes accessed | tf_op | source)
XLA Modules:
  0.0 60.9 jit_solution(308012517682691200)
XLA Ops:
  0.0 1.0 %send.1 = bf16[400,128]{1,0:T(8,128)(2,1)S(1)} custom-call(bf16[2,160,160]{2,1,0:T(8,128)(2,1)} %couplings.3), custom_call_target="tpu_custom_call" | custom-call | tf_op jit(solution)/shard_map/send/pallas_call | solution.py:161
  1.0 1.3 %collective-permute-start.1 = (bf16[400,128]{1,0:T(8,128)(2,1)S(1)}, bf16[400,128]{1,0:T(8,128)(2,1)S(1)}, u32[]{:S(2)}, u32[]{:S(2)}) collective-permute-start(bf16[400,128]{1,0:T(8,128)(2,1)S(1)} %send.1), channel_id=1, source_target_pairs={{12,0},{14,2},{16,4},{18,6},{20,8},{22,10},{13,1},{15,3},{17,5},{1... | collective-permute-start | bytes 307208 | tf_op jit(solution)/shard_map/ppermute | solution.py:170
  2.3 14.2 %collective-permute-start = (bf16[400,128]{1,0:T(8,128)(2,1)S(1)}, bf16[400,128]{1,0:T(8,128)(2,1)S(1)}, u32[]{:S(2)}, u32[]{:S(2)}) collective-permute-start(bf16[400,128]{1,0:T(8,128)(2,1)S(1)} %send.1), channel_id=1, source_target_pairs={{0,12},{2,14},{4,16},{6,18},{8,20},{10,22},{1,13},{3,15},{5,17},{7... | collective-permute-start | bytes 307208 | tf_op jit(solution)/shard_map/ppermute | solution.py:171
  16.6 1.5 %direct.1 = (bf16[400,128]{1,0:T(8,128)(2,1)S(1)}, bf16[4,160,160]{2,1,0:T(8,128)(2,1)S(1)}, bf16[4,160,160]{2,1,0:T(8,128)(2,1)S(1)}, s32[8,128]{1,0:T(8,128)S(1)}) custom-call(s32[2,2]{1,0:T(2,128)} %blocks.1, s32[2]{0:T(128)} %partner.1, bf16[6,160,160]{2,1,0:T(8,128)(2,1)} %bitcast.8, bf16[2,160,160]{2,1,0:T(8,128)(2,1)} %couplings.3), custom_call_target="tpu_custom_call" | custom-call | tf_op jit(solution)/shard_map/direct/pallas_call | solution.py:174
  18.1 1.7 %collective-permute-done.1 = bf16[400,128]{1,0:T(8,128)(2,1)S(1)} collective-permute-done((bf16[400,128]{1,0:T(8,128)(2,1)S(1)}, bf16[400,128]{1,0:T(8,128)(2,1)S(1)}, u32[]{:S(2)}, u32[]{:S(2)}) %collective-permute-start.1) | collective-permute-done | bytes 102432 | tf_op jit(solution)/shard_map/ppermute | solution.py:170
  19.8 25.3 %conditional.2 = (bf16[512,128]{1,0:T(8,128)(2,1)S(1)}) conditional(s32[]{:T(128)} %convert_element_type.4, () %tuple.18, (bf16[4,160,160]{2,1,0:T(8,128)(2,1)S(1)}, s32[8,128]{1,0:T(8,128)S(1)}, bf16[400,128]{1,0:T(8,128)(2,1)S(1)}, bf16[400,128]{1,0:T(8,128)(2,1)S(1)}) %tuple.19), branch_computations={%region_0.0_spmd, %region_1.0_spmd} | conditional | bytes 524296 | solution.py:205
  19.8 0.6 mirror.2
  20.4 24.1 %all_to_all.13.incoming = bf16[64,16,128]{2,1,0:T(8,128)(2,1)S(1)} all-to-all(bf16[64,16,128]{2,1,0:T(8,128)(2,1)S(1)} %mirror.2), channel_id=1, replica_groups=mesh['x'=4,'inside'=8,'pair'=12,'sub'=2] {'inside','sub','x'}, dimensions={0} | all-to-all | bytes 524288 | tf_op jit(solution)/shard_map/cond/branch_1_fun/all_to_all | solution.py:191
  44.5 0.6 convolve.2
  45.1 0.0 collective-permute-done
  45.1 14.7 %all_to_all.15 = bf16[64,8,128]{2,1,0:T(8,128)(2,1)S(1)} all-to-all(bf16[64,8,128]{2,1,0:T(8,128)(2,1)S(1)} %bitcast.7), channel_id=1, replica_groups=mesh['x'=4,'inside'=8,'pair'=12,'sub'=2] {'inside','sub','x'}, dimensions={0} | all-to-all | bytes 262144 | tf_op jit(solution)/shard_map/all_to_all | solution.py:207
  59.8 1.1 %screen.1 = bf16[2,160,160]{2,1,0:T(8,128)(2,1)} custom-call(bf16[4,160,160]{2,1,0:T(8,128)(2,1)S(1)} %get-tuple-element.40.factors, bf16[512,128]{1,0:T(8,128)(2,1)S(1)} %bitcast.6), custom_call_target="tpu_custom_call" | custom-call | tf_op jit(solution)/shard_map/screen/pallas_call | solution.py:210
  (1 shorter events, 0.0 us)
Async XLA Ops:
  1.0 18.8 %collective-permute-start.1 = (bf16[400,128]{1,0:T(8,128)(2,1)S(1)}, bf16[400,128]{1,0:T(8,128)(2,1)S(1)}, u32[]{:S(2)}, u32[]{:S(2)}) collective-permute-start(bf16[400,128]{1,0:T(8,128)(2,1)S(1)} %send.1), channel_id=1, source_target_pairs={{12,0},{14,2},{16,4},{18,6},{20,8},{22,10},{13,1},{15,3},{17,5},{1... | collective-permute-start | bytes 307208 | tf_op jit(solution)/shard_map/ppermute | solution.py:170
  2.3 42.8 %collective-permute-start = (bf16[400,128]{1,0:T(8,128)(2,1)S(1)}, bf16[400,128]{1,0:T(8,128)(2,1)S(1)}, u32[]{:S(2)}, u32[]{:S(2)}) collective-permute-start(bf16[400,128]{1,0:T(8,128)(2,1)S(1)} %send.1), channel_id=1, source_target_pairs={{0,12},{2,14},{4,16},{6,18},{8,20},{10,22},{1,13},{3,15},{5,17},{7... | collective-permute-start | bytes 307208 | tf_op jit(solution)/shard_map/ppermute | solution.py:171

commit v2 on v1

--- a/solution.py
+++ b/solution.py
@@ -103,7 +103,7 @@
     out[used:] = jnp.zeros((out.shape[0] - used, 2 * ROWS, LANES), jnp.bfloat16)
 
 
-def convolve_kernel(tile, inner, incoming, out, first, second):
+def convolve_kernel(tile, inside, subs, incoming, out, first, second):
     count = incoming.shape[0]
     both = incoming[...].astype(jnp.float32)
     first[...] = both[:, :ROWS]
@@ -111,7 +111,9 @@
     scale = count ** (-0.5)
 
     def slot(energy):
-        return energy % inner * (count // inner) + energy // inner
+        rest, sub = divmod(energy, subs)
+        x, place = divmod(rest, inside)
+        return (place * (count // (inside * subs)) + x) * subs + sub
 
     for e0 in range(0, count, tile):
         totals = [None] * tile
@@ -129,9 +131,9 @@
                         continue
                     term = lhs[dt] * other
                     totals[de] = term if totals[de] is None else totals[de] + term
-        for de in range(tile):
-            total = (totals[de] * scale).astype(jnp.bfloat16)
-            out[pl.ds(slot(e0 + de) * ROWS, ROWS), :] = total
+        for de in range(0, tile, 2):
+            pair = jnp.concatenate([totals[de], totals[de + 1]], axis=0) * scale
+            out[pl.ds(slot(e0 + de) * ROWS, 2 * ROWS), :] = pair.astype(jnp.bfloat16)
 
 
 def screen_kernel(factors, packed, out, held, sems):
@@ -152,7 +154,7 @@
 
 
 def per_device(orbitals, couplings, blocks, partner):
-    axes = ("inside", "sub", "x")
+    axes = ("inside", "x", "sub")
     energies = lax.axis_size(axes)
     pairs = lax.axis_size("pair")
     order = couplings.shape[1]
@@ -190,7 +192,9 @@
         )(onchip(arriving), onchip(crossed), onchip(shifted), onchip(direct))
         incoming = lax.all_to_all(outgoing, axes, split_axis=0, concat_axis=0, tiled=True)
         return pl.pallas_call(
-            functools.partial(convolve_kernel, 8, energies // lax.axis_size("x")),
+            functools.partial(
+                convolve_kernel, 8, lax.axis_size("inside"), lax.axis_size("sub")
+            ),
             out_shape=result,
             in_specs=[VMEM],
             out_specs=VMEM,

time: 61.1 us -> 61.1 us (level)
  no operation moved by 1% of the time
where the time goes in v2:
time: 61.1 us; the launch traced here: 60.9 us
  blocking collectives  38.8 us (64%)
  starting transfers between devices  15.5 us (25%)
  Pallas kernels  4.76 us (8%)
  waiting for transfers between devices  1.73 us (3%)
    all_to_all x1, blocking collectives, polarize(): lax.all_to_all(outgoing, axes, split_axis=0, concat_axis=0, tiled=True)  24 us
    all_to_all x1, blocking collectives, per_device(): lax.all_to_all(polar.reshape(energies, ROWS, LANES), axes, split_axis=0,...  14.8 us
    ppermute x1, starting transfers between devices, per_device(): lax.ppermute(leaving, 'pair', [(i, i + near) for i in range(near)])  14.2 us
    ppermute x1, waiting for transfers between devices, per_device(): lax.ppermute(leaving, 'pair', [(i + near, i) for i in range(near)])  1.73 us
    pallas_call x1, Pallas kernels, per_device(): pl.pallas_call(direct_kernel, out_shape=[packed, chosen, chosen, pltpu.VM...  1.48 us
    ppermute x1, starting transfers between devices, per_device(): lax.ppermute(leaving, 'pair', [(i + near, i) for i in range(near)])  1.29 us
  transfers between devices with their start and end apart: 2, of which 1 were waited for; matrix products, arithmetic and copies ran while one was open for 0% of the time, Pallas kernels for 4%

profile of v2, /device:TPU:64, one launch (start us, length us, event | category | flops | bytes accessed | tf_op | source)
XLA Modules:
  0.0 60.9 jit_solution(15512617979336983860)
XLA Ops:
  0.0 1.0 %send.1 = bf16[400,128]{1,0:T(8,128)(2,1)S(1)} custom-call(bf16[2,160,160]{2,1,0:T(8,128)(2,1)} %couplings.3), custom_call_target="tpu_custom_call" | custom-call | tf_op jit(solution)/shard_map/send/pallas_call | solution.py:163
  1.0 1.3 %collective-permute-start.1 = (bf16[400,128]{1,0:T(8,128)(2,1)S(1)}, bf16[400,128]{1,0:T(8,128)(2,1)S(1)}, u32[]{:S(2)}, u32[]{:S(2)}) collective-permute-start(bf16[400,128]{1,0:T(8,128)(2,1)S(1)} %send.1), channel_id=1, source_target_pairs={{12,0},{14,2},{16,4},{18,6},{20,8},{22,10},{13,1},{15,3},{17,5},{1... | collective-permute-start | bytes 307208 | tf_op jit(solution)/shard_map/ppermute | solution.py:172
  2.3 14.2 %collective-permute-start = (bf16[400,128]{1,0:T(8,128)(2,1)S(1)}, bf16[400,128]{1,0:T(8,128)(2,1)S(1)}, u32[]{:S(2)}, u32[]{:S(2)}) collective-permute-start(bf16[400,128]{1,0:T(8,128)(2,1)S(1)} %send.1), channel_id=1, source_target_pairs={{0,12},{2,14},{4,16},{6,18},{8,20},{10,22},{1,13},{3,15},{5,17},{7... | collective-permute-start | bytes 307208 | tf_op jit(solution)/shard_map/ppermute | solution.py:173
  16.6 1.5 %direct.1 = (bf16[400,128]{1,0:T(8,128)(2,1)S(1)}, bf16[4,160,160]{2,1,0:T(8,128)(2,1)S(1)}, bf16[4,160,160]{2,1,0:T(8,128)(2,1)S(1)}, s32[8,128]{1,0:T(8,128)S(1)}) custom-call(s32[2,2]{1,0:T(2,128)} %blocks.1, s32[2]{0:T(128)} %partner.1, bf16[6,160,160]{2,1,0:T(8,128)(2,1)} %bitcast.8, bf16[2,160,160]{2,1,0:T(8,128)(2,1)} %couplings.3), custom_call_target="tpu_custom_call" | custom-call | tf_op jit(solution)/shard_map/direct/pallas_call | solution.py:176
  18.1 1.7 %collective-permute-done.1 = bf16[400,128]{1,0:T(8,128)(2,1)S(1)} collective-permute-done((bf16[400,128]{1,0:T(8,128)(2,1)S(1)}, bf16[400,128]{1,0:T(8,128)(2,1)S(1)}, u32[]{:S(2)}, u32[]{:S(2)}) %collective-permute-start.1) | collective-permute-done | bytes 102432 | tf_op jit(solution)/shard_map/ppermute | solution.py:172
  19.8 25.2 %conditional.2 = (bf16[512,128]{1,0:T(8,128)(2,1)S(1)}) conditional(s32[]{:T(128)} %convert_element_type.4, () %tuple.18, (bf16[4,160,160]{2,1,0:T(8,128)(2,1)S(1)}, s32[8,128]{1,0:T(8,128)S(1)}, bf16[400,128]{1,0:T(8,128)(2,1)S(1)}, bf16[400,128]{1,0:T(8,128)(2,1)S(1)}) %tuple.19), branch_computations={%region_0.0_spmd, %region_1.0_spmd} | conditional | bytes 524296 | solution.py:209
  19.8 0.6 mirror.2
  20.4 24.0 %all_to_all.13.incoming = bf16[64,16,128]{2,1,0:T(8,128)(2,1)S(1)} all-to-all(bf16[64,16,128]{2,1,0:T(8,128)(2,1)S(1)} %mirror.2), channel_id=1, replica_groups=mesh['x'=4,'inside'=8,'pair'=12,'sub'=2] {'inside','x','sub'}, dimensions={0} | all-to-all | bytes 524288 | tf_op jit(solution)/shard_map/cond/branch_1_fun/all_to_all | solution.py:193
  44.4 0.6 convolve.2
  45.0 0.0 collective-permute-done
  45.0 14.8 %all_to_all.15 = bf16[64,8,128]{2,1,0:T(8,128)(2,1)S(1)} all-to-all(bf16[64,8,128]{2,1,0:T(8,128)(2,1)S(1)} %bitcast.7), channel_id=1, replica_groups=mesh['x'=4,'inside'=8,'pair'=12,'sub'=2] {'inside','x','sub'}, dimensions={0} | all-to-all | bytes 262144 | tf_op jit(solution)/shard_map/all_to_all | solution.py:211
  59.8 1.1 %screen.1 = bf16[2,160,160]{2,1,0:T(8,128)(2,1)} custom-call(bf16[4,160,160]{2,1,0:T(8,128)(2,1)S(1)} %get-tuple-element.40.factors, bf16[512,128]{1,0:T(8,128)(2,1)S(1)} %bitcast.6), custom_call_target="tpu_custom_call" | custom-call | tf_op jit(solution)/shard_map/screen/pallas_call | solution.py:214
  (1 shorter events, 0.0 us)
Async XLA Ops:
  1.0 18.8 %collective-permute-start.1 = (bf16[400,128]{1,0:T(8,128)(2,1)S(1)}, bf16[400,128]{1,0:T(8,128)(2,1)S(1)}, u32[]{:S(2)}, u32[]{:S(2)}) collective-permute-start(bf16[400,128]{1,0:T(8,128)(2,1)S(1)} %send.1), channel_id=1, source_target_pairs={{12,0},{14,2},{16,4},{18,6},{20,8},{22,10},{13,1},{15,3},{17,5},{1... | collective-permute-start | bytes 307208 | tf_op jit(solution)/shard_map/ppermute | solution.py:172
  2.3 42.7 %collective-permute-start = (bf16[400,128]{1,0:T(8,128)(2,1)S(1)}, bf16[400,128]{1,0:T(8,128)(2,1)S(1)}, u32[]{:S(2)}, u32[]{:S(2)}) collective-permute-start(bf16[400,128]{1,0:T(8,128)(2,1)S(1)} %send.1), channel_id=1, source_target_pairs={{0,12},{2,14},{4,16},{6,18},{8,20},{10,22},{1,13},{3,15},{5,17},{7... | collective-permute-start | bytes 307208 | tf_op jit(solution)/shard_map/ppermute | solution.py:173
